TPU v7x, 32 devices: a whole 2x2x4 slice. The times are simulated.
32 devices in a mesh: seq: 8 (over z, x), exp: 4 (over y, core).
Axes of the slice: x: 2, y: 2, z: 4, core: 2. Of those that a mesh axis runs over, the one named last changes fastest.
Arguments:
- residual: bfloat16 [4096, 8192], P('seq', 'exp'), may hold values from -16 to 16
- queries: bfloat16 [4096, 4096], P('seq', 'exp'), may hold values from -6 to 6
- keys: bfloat16 [4096, 4096], P('seq', 'exp'), may hold values from -10 to 10
- values: bfloat16 [4096, 4096], P('seq', 'exp'), may hold values from -6 to 6
- documents: int32 [4096], replicated, may hold values from 0 to 1, as said below
- out_proj: bfloat16 [4096, 8192], P(None, 'exp'), may hold values from -0.09375 to 0.09375
- modality: int32 [4096], P('seq'), may hold values from 0 to 1, as said below
- norm_gain: float32 [2, 8192], P(None, 'exp'), may hold values from 0.25 to 1.75
- picks: int32 [4, 64], replicated, may hold values from 0 to 4095, as said below
- router: bfloat16 [8192, 4], P(None, 'exp'), may hold values from -0.0625 to 0.0625
- w_gate: bfloat16 [4, 8192, 4096], P('exp', None, 'seq'), may hold values from -0.0625 to 0.0625
- w_up: bfloat16 [4, 8192, 4096], P('exp', None, 'seq'), may hold values from -0.0625 to 0.0625
- w_down: bfloat16 [4, 4096, 8192], P('exp', 'seq'), may hold values from -0.09375 to 0.09375
Outputs:
- layer_out: bfloat16 [4096, 8192], P('seq', 'exp')
Inputs may be any that keep to these rules, and one draw needn't show every extreme that they name: `modality`: 0 marks a text token, 1 an image token. `documents`: 0 for the first document, 1 for the second; the second begins between position 1024 and 3072. `picks`: row e lists 64 different positions in ascending order; all carry modality 0 for e < 2 and modality 1 otherwise. Within each aligned block of 512 positions (the tokens of one index of seq) a row lists at most 16 positions, and every row lists exactly 16 in some block.
All inputs are finite; a program needn't handle non-finite values.
Results may differ from a plain program's by a relative error of at most 0.0035.
Values may be sent and summed in bfloat16 or wider, within the bound.
A program may use at most 128 MiB of HBM per device.

v0:
```python
import math
import jax
import jax.numpy as jnp
from jax import lax
from jax.sharding import PartitionSpec as P

D = 8192
HD = 128
block_rows = 512


def shards(
    residual,
    queries,
    keys,
    values,
    documents,
    out_proj,
    modality,
    norm_gain,
    picks,
    router,
    w_gate,
    w_up,
    w_down,
):
    tokens = queries.shape[0]
    heads_here = queries.shape[1] // HD
    seq_pos = lax.axis_index("seq")
    start_row = seq_pos * tokens
    query_pos = start_row + jnp.arange(tokens, dtype=jnp.int32)
    query_doc = lax.dynamic_slice_in_dim(documents, start_row, tokens, 0)
    query_heads = queries.reshape(tokens, heads_here, HD)
    score_scale = 1.0 / math.sqrt(HD)

    def attend(state, key_rows, value_rows, key_start):
        row_count = key_rows.shape[0]
        key_pos = key_start + jnp.arange(row_count, dtype=jnp.int32)
        key_doc = lax.dynamic_slice_in_dim(documents, key_start, row_count, 0)
        scores = (
            jnp.einsum(
                "qhd,khd->qhk",
                query_heads,
                key_rows.reshape(row_count, heads_here, HD),
                preferred_element_type=jnp.float32,
            )
            * score_scale
        )
        allowed = (key_pos[None, :] <= query_pos[:, None]) & (
            key_doc[None, :] == query_doc[:, None]
        )
        scores = jnp.where(allowed[:, None, :], scores, -jnp.inf)
        running_max, running_sum, running_out = state
        new_max = jnp.maximum(running_max, jnp.max(scores, axis=2))
        factor = jnp.exp(running_max - new_max)
        weights = jnp.exp(scores - new_max[:, :, None])
        running_sum = running_sum * factor + jnp.sum(weights, axis=2)
        running_out = running_out * factor[:, :, None] + jnp.einsum(
            "qhk,khd->qhd",
            weights.astype(jnp.bfloat16),
            value_rows.reshape(row_count, heads_here, HD),
            preferred_element_type=jnp.float32,
        )
        return (new_max, running_sum, running_out)

    def visit_block(state, key_rows, value_rows, key_start):
        row_count = key_rows.shape[0]
        last_doc = lax.dynamic_index_in_dim(documents, key_start + row_count - 1, 0, keepdims=False)
        beyond = (key_start > query_pos[tokens - 1]) | (last_doc < query_doc[0])
        return lax.cond(
            beyond,
            lambda inner_state: inner_state,
            lambda inner_state: attend(inner_state, key_rows, value_rows, key_start),
            state,
        )

    initial = (
        jnp.full((tokens, heads_here), -1e30, jnp.float32),
        jnp.zeros((tokens, heads_here), jnp.float32),
        jnp.zeros((tokens, heads_here, HD), jnp.float32),
    )
    state = initial
    key_piece = lax.all_gather(keys, "seq", axis=0, tiled=True)
    value_piece = lax.all_gather(values, "seq", axis=0, tiled=True)
    row_count = key_piece.shape[0]
    blocks = row_count // block_rows
    key_stack = key_piece.reshape(blocks, block_rows, key_piece.shape[1])
    value_stack = value_piece.reshape(blocks, block_rows, value_piece.shape[1])

    def scan_step(inner_state, block_item):
        block_index, key_rows, value_rows = block_item
        return (visit_block(inner_state, key_rows, value_rows, block_index * block_rows), None)

    state, unused = lax.scan(
        scan_step, state, (jnp.arange(blocks, dtype=jnp.int32), key_stack, value_stack)
    )
    running_max, running_sum, running_out = state
    attended = (
        (running_out / running_sum[:, :, None])
        .reshape(tokens, heads_here * HD)
        .astype(jnp.bfloat16)
    )
    mixed = jnp.dot(
        lax.all_gather(attended, "exp", axis=1, tiled=True),
        out_proj,
        preferred_element_type=jnp.float32,
    )
    hidden_state = (residual.astype(jnp.float32) + mixed).astype(jnp.bfloat16)
    hidden_wide = hidden_state.astype(jnp.float32)
    square_total = lax.psum(jnp.sum(hidden_wide * hidden_wide, axis=1), "exp")
    inverse = lax.rsqrt(square_total / D + 1e-05)
    gain_rows = jnp.where(modality[:, None] == 0, norm_gain[0][None, :], norm_gain[1][None, :])
    normed = (hidden_wide * inverse[:, None] * gain_rows).astype(jnp.bfloat16)
    capacity = tokens // 32
    inside = (picks >= start_row) & (picks < start_row + tokens)
    slot_index = jnp.cumsum(inside.astype(jnp.int32), axis=1) - 1
    matched = inside[:, None, :] & (
        slot_index[:, None, :] == jnp.arange(capacity, dtype=jnp.int32)[None, :, None]
    )
    local_index = jnp.sum(jnp.where(matched, picks[:, None, :] - start_row, 0), axis=2)
    filled = jnp.any(matched, axis=2)
    rows_out = jnp.take(normed, local_index.T, axis=0)
    rows_out = jnp.where(filled.T[:, :, None], rows_out, jnp.zeros_like(rows_out))
    arrived = lax.all_to_all(rows_out, "exp", split_axis=1, concat_axis=1, tiled=True)
    expert_rows = arrived.reshape(capacity, D)
    logits = jnp.dot(expert_rows, router, preferred_element_type=jnp.float32)[:, 0]
    piece = lax.all_gather(expert_rows, "seq", axis=0, tiled=True)
    gate_part = jnp.dot(piece, w_gate[0], preferred_element_type=jnp.float32)
    up_part = jnp.dot(piece, w_up[0], preferred_element_type=jnp.float32)
    inner_act = (jax.nn.silu(gate_part) * up_part).astype(jnp.bfloat16)
    summed = lax.psum_scatter(
        jnp.dot(inner_act, w_down[0], preferred_element_type=jnp.float32).astype(jnp.bfloat16),
        "seq",
        scatter_dimension=0,
        tiled=True,
    ).astype(jnp.float32)
    weighted = (jax.nn.sigmoid(logits)[:, None] * summed).astype(jnp.bfloat16)
    own_expert = lax.axis_index("exp")
    own_index = lax.dynamic_index_in_dim(local_index, own_expert, 0, keepdims=False)
    own_filled = lax.dynamic_index_in_dim(filled, own_expert, 0, keepdims=False)
    placing = (
        (jnp.arange(tokens, dtype=jnp.int32)[:, None] == own_index[None, :]) & own_filled[None, :]
    ).astype(jnp.bfloat16)
    spread = jnp.dot(placing, weighted, preferred_element_type=jnp.float32)
    expert_add = lax.psum_scatter(
        spread.astype(jnp.bfloat16), "exp", scatter_dimension=1, tiled=True
    ).astype(jnp.float32)
    return (hidden_wide + expert_add).astype(jnp.bfloat16)


def solution(mesh):
    return jax.shard_map(
        shards,
        mesh=mesh,
        in_specs=(
            P("seq", "exp"),
            P("seq", "exp"),
            P("seq", "exp"),
            P("seq", "exp"),
            P(),
            P(None, "exp"),
            P("seq"),
            P(None, "exp"),
            P(),
            P(None, "exp"),
            P("exp", None, "seq"),
            P("exp", None, "seq"),
            P("exp", "seq", None),
        ),
        out_specs=P("seq", "exp"),
        check_vma=False,
    )
```

profile of v0, /device:TPU:0, one launch (start us, length us, event | category | flops | bytes accessed | tf_op | source)
XLA Modules:
  0.0 667.6 jit_solution(14505423510101249050)
XLA Ops:
  6.5 0.7 all-gather.5.cloned.1.call-update
  7.3 0.7 all-gather.7.cloned.1.call-update
  8.1 1.5 copy.56
  9.6 0.7 copy.58
  10.2 0.8 dynamic_slice.55
  11.0 125.7 %all-gather.5.cloned.1.call-done = bf16[4096,1024]{1,0:T(8,128)(2,1)} async-done(((bf16[512,1024]{1,0:T(8,128)(2,1)}), bf16[4096,1024]{1,0:T(8,128)(2,1)}) %all-gather.5.cloned.1.call-update) | async-done | bytes 8388624 | tf_op jit(solution)/shard_map/all_gather | solution.py:83
  136.7 11.6 %copy.57 = bf16[8,512,1024]{1,2,0:T(8,128)(2,1)} copy(bf16[8,512,1024]{2,1,0:T(8,128)(2,1)} %bitcast.77) | data formatting | bytes 16777216 | tf_op jit(solution)/shard_map/while | solution.py:94
  148.3 113.2 %all-gather.7.cloned.1.call-done = bf16[4096,1024]{1,0:T(8,128)(2,1)} async-done(((bf16[512,1024]{1,0:T(8,128)(2,1)}), bf16[4096,1024]{1,0:T(8,128)(2,1)}) %all-gather.7.cloned.1.call-update) | async-done | bytes 8388624 | tf_op jit(solution)/shard_map/all_gather | solution.py:84
  261.5 11.4 %copy.59 = bf16[8,512,1024]{1,2,0:T(8,128)(2,1)} copy(bf16[8,512,1024]{2,1,0:T(8,128)(2,1)} %bitcast.78) | data formatting | bytes 16777216 | tf_op jit(solution)/shard_map/while | solution.py:94
  273.1 55.4 %while.18 = (s32[]{:T(128)}, f32[512,8]{0,1:T(8,128)S(1)}, f32[512,8]{0,1:T(8,128)S(1)}, f32[512,8,128]{2,0,1:T(8,128)S(1)}, s32[8]{0:T(128)S(1)}, /*index=5*/s3...) while((s32[]{:T(128)}, f32[512,8]{0,1:T(8,128)S(1)}, ...), condition=%wide.region_5.6_spmd, body=%wide.region_0.5_spmd.sunk | while | flops 1098654208 | bytes 38025672 | solution.py:94
  273.1 0.6 dynamic_slice.64
  274.4 1.3 dynamic_slice.65
  275.6 0.6 slice.33
  277.5 0.6 slice.32
  278.7 9.6 %conditional.2 = (f32[512,8]{0,1:T(8,128)S(1)}, f32[512,8]{0,1:T(8,128)S(1)}, f32[512,8,128]{2,0,1:T(8,128)S(1)}) conditional(s32[]{:T(128)} %convert_element_type.103, (s32[]{:T(128)}, s32[512]{0:T(512)S(1)}, s32[4096]{0:T(1024)}, s32[512]{0:T(512)S(1)}, bf16[8,512,1024]{1,2,0:T(8,128)(2,1)}, /*index=5*/s32[]{:T(128)}, ...), branch_computations={%region_1.3_spmd, %region_4.4_spmd} | conditional | flops 1098654208 | bytes 37992520 | solution.py:70
  278.8 0.8 dynamic_slice.47
  279.8 1.7 constant_dynamic-slice_fusion
  281.5 1.7 fusion.2
  283.2 1.7 fusion.1
  285.0 3.4 bitcast_add_fusion
  288.4 0.6 dynamic_slice.64
  289.6 1.3 dynamic_slice.65
  290.9 0.6 slice.33
  292.8 0.6 slice.32
  294.1 0.6 dynamic_slice.64
  295.4 1.3 dynamic_slice.65
  296.7 0.6 slice.33
  298.5 0.6 slice.32
  299.8 0.6 dynamic_slice.64
  301.1 1.3 dynamic_slice.65
  302.4 0.6 slice.33
  304.3 0.6 slice.32
  305.6 0.6 dynamic_slice.64
  306.8 1.3 dynamic_slice.65
  308.1 0.6 slice.33
  310.0 0.6 slice.32
  311.3 0.6 dynamic_slice.64
  312.6 1.3 dynamic_slice.65
  313.9 0.6 slice.33
  315.7 0.6 slice.32
  317.0 0.6 dynamic_slice.64
  318.3 1.3 dynamic_slice.65
  319.6 0.6 slice.33
  321.5 0.6 slice.32
  322.8 0.6 dynamic_slice.64
  324.0 1.3 dynamic_slice.65
  325.3 0.6 slice.33
  327.2 0.6 slice.32
  328.5 1.8 copy.60
  330.3 2.8 divide_convert_fusion
  334.3 79.5 %all-gather.9.cloned.1.call-done = bf16[512,4096]{0,1:T(8,128)(2,1)} async-done(((bf16[512,1024]{0,1:T(8,128)(2,1)}), bf16[512,4096]{0,1:T(8,128)(2,1)}) %all-gather.9.cloned.1.call-update) | async-done | bytes 4194320 | tf_op jit(solution)/shard_map/all_gather | solution.py:104
  413.8 14.2 %fusion.18 = (f32[512]{0:T(512)S(1)}, bf16[512,2048]{1,0:T(8,128)(2,1)S(1)}) fusion(bf16[512,4096]{0,1:T(8,128)(2,1)} %all-gather.9.cloned.1.call-done, bf16[4096,2048]{1,0:T(8,128)(2,1)} %param.22, bf16[512,2048]{1,0:T(8,128)(2,1)} %param.17), kind=kOutput, calls=%fused_computation.30 | convolution fusion | flops 8596226048 | bytes 25167872 | tf_op jit(solution)/shard_map/dot_general | solution.py:103
  428.0 5.9 psum.7
  433.9 2.1 fusion.20
  436.0 2.8 gather_fusion
  439.3 8.7 %all_to_all.5 = bf16[16,4,2048]{2,0,1:T(8,128)(2,1)S(1)} all-to-all(bf16[16,4,2048]{2,0,1:T(8,128)(2,1)S(1)} %fusion.34), channel_id=1, replica_groups=mesh['seq'=8,'exp'=4] {'exp'}, dimensions={1} | all-to-all | bytes 524288 | tf_op jit(solution)/shard_map/all_to_all | solution.py:124
  448.0 0.7 copy.67
  448.8 49.2 %all-gather.11.cloned.1.call-done = bf16[128,8192]{1,0:T(8,128)(2,1)} async-done(((bf16[16,8192]{1,0:T(8,128)(2,1)}), bf16[128,8192]{1,0:T(8,128)(2,1)}) %all-gather.11.cloned.1.call-update) | async-done | bytes 2097168 | tf_op jit(solution)/shard_map/all_gather | solution.py:127
  498.0 5.4 fusion.16
  503.5 9.6 %convolution_convert_fusion.1 = bf16[128,8192]{1,0:T(8,128)(2,1)} fusion(bf16[1,512,8192]{2,1,0:T(8,128)(2,1)} %param.29, bf16[128,8192]{1,0:T(8,128)(2,1)S(1)} %copy-done.1, bf16[1,8192,512]{2,1,0:T(8,128)(2,1)} %param.28, f32[128,512]{1,0:T(8,128)S(1)} %fusion.16), kind=kOutput, calls=%fused_computation.21 | convolution fusion | flops 2148925440 | bytes 21233664 | tf_op jit(solution)/shard_map/dot_general | solution.py:132
  513.6 66.4 %reduce-scatter.3.cloned.1.call-done = bf16[16,8192]{1,0:T(8,128)(2,1)} async-done(((bf16[128,8192]{1,0:T(8,128)(2,1)}), bf16[16,8192]{1,0:T(8,128)(2,1)}) %reduce-scatter.3.cloned.1.call-update) | async-done | bytes 262160 | tf_op jit(solution)/shard_map/reduce_scatter | solution.py:131
  580.1 6.6 convolution_convert_fusion
  586.7 70.4 %reduce-scatter.5.cloned.1.call-done = bf16[512,2048]{1,0:T(8,128)(2,1)} async-done(((bf16[512,8192]{1,0:T(8,128)(2,1)}), bf16[512,2048]{1,0:T(8,128)(2,1)}) %reduce-scatter.5.cloned.1.call-update) | async-done | bytes 2097168 | tf_op jit(solution)/shard_map/reduce_scatter | solution.py:145
  657.1 3.7 fusion.21
  (75 shorter events, 2.9 us)
Async XLA Ops:
  6.5 506.9 %copy-start = (bf16[8192,1]{0,1:T(2,128)(2,1)S(1)}, bf16[8192,1]{0,1:T(2,128)(2,1)}, u32[]{:S(2)}) copy-start(bf16[8192,1]{0,1:T(2,128)(2,1)} %param.26) | copy-start | bytes 49156
  6.5 130.1 %all-gather.5.cloned.1.call-start = ((), (), s32[]{:S(2)}) async-start(), calls=%async_computation.3 | async-start | bytes 9437184 | tf_op jit(solution)/shard_map/all_gather | solution.py:83
  7.3 254.2 %all-gather.7.cloned.1.call-start = ((), (), s32[]{:S(2)}) async-start(), calls=%async_computation.4 | async-start | bytes 9437184 | tf_op jit(solution)/shard_map/all_gather | solution.py:84
  8.0 405.8 %all-gather.9.cloned.1.call-start = ((), (), s32[]{:S(2)}) async-start(), calls=%async_computation.5 | async-start | bytes 5242880 | tf_op jit(solution)/shard_map/all_gather | solution.py:104
  328.5 4.9 copy-start.6
  328.5 5.7 copy-start.7
  328.5 5.7 copy-start.5
  333.2 164.8 %all-gather.11.cloned.1.call-start = ((), (), s32[]{:S(2)}) async-start(), calls=%async_computation.6 | async-start | bytes 2359296 | tf_op jit(solution)/shard_map/all_gather | solution.py:127
  428.0 20.8 %copy-start.2 = (bf16[512,2048]{1,0:T(8,128)(2,1)}, bf16[512,2048]{1,0:T(8,128)(2,1)S(1)}, u32[]{:S(2)}) copy-start(bf16[512,2048]{1,0:T(8,128)(2,1)S(1)} %get-tuple-element.425) | copy-start | bytes 6291460
  448.8 131.3 %reduce-scatter.3.cloned.1.call-start = ((), (), s32[]{:S(2)}) async-start(), calls=%async_computation.7 | async-start | bytes 2359296 | tf_op jit(solution)/shard_map/reduce_scatter | solution.py:131
  498.0 5.4 copy-start.1
  503.5 10.0 %copy-start.4 = (bf16[4,2,8,2048]{3,2,0,1:T(8,128)(2,1)S(1)}, bf16[4,2,8,2048]{3,2,0,1:T(8,128)(2,1)}, u32[]{:S(2)}) copy-start(bf16[4,2,8,2048]{3,2,0,1:T(8,128)(2,1)} %copy.67) | copy-start | bytes 786436
  513.1 144.0 %reduce-scatter.5.cloned.1.call-start = ((), (), s32[]{:S(2)}) async-start(), calls=%async_computation.8 | async-start | bytes 10485760 | tf_op jit(solution)/shard_map/reduce_scatter | solution.py:145
  586.6 70.5 %copy-start.3 = (bf16[512,2048]{1,0:T(8,128)(2,1)S(1)}, bf16[512,2048]{1,0:T(8,128)(2,1)}, u32[]{:S(2)}) copy-start(bf16[512,2048]{1,0:T(8,128)(2,1)} %copy-done.2) | copy-start | bytes 6291460
Sparse Core Ops, SparseCore 0:
  9.5 127.1 all-gather.4
  138.8 122.6 all-gather.6
  333.3 80.4 all-gather.8
  448.9 49.0 all-gather.10
  513.2 66.7 reduce-scatter.2
  586.8 70.2 reduce-scatter.4
where the time goes:
time: 669 us; the launch traced here: 668 us
  waiting for transfers between devices  506 us (76%)
  local copies, waits for them, and re-layouts  59.3 us (9%)
  matrix products  41 us (6%)
  loops' own time  20.9 us (3%)
  blocking collectives  14.6 us (2%)
  between operations  13.7 us (2%)
  other arithmetic  11.6 us (2%)
    all_gather x1, waiting for transfers between devices, shards(): key_piece = lax.all_gather(keys, 'seq', axis=0, tiled=True)  126 us
    all_gather x1, waiting for transfers between devices, shards(): value_piece = lax.all_gather(values, 'seq', axis=0, tiled=True)  113 us
    all_gather x1, waiting for transfers between devices, shards(): lax.all_gather(attended, 'exp', axis=1, tiled=True)  79.5 us
    reduce_scatter x1, waiting for transfers between devices, shards(): lax.psum_scatter(spread.astype(jnp.bfloat16), 'exp', scatter_dimension=1,...  70.4 us
    reduce_scatter x1, waiting for transfers between devices, shards(): lax.psum_scatter(jnp.dot(inner_act, w_down[0], preferred_element_type=jnp...  66.4 us
    all_gather x1, waiting for transfers between devices, shards(): piece = lax.all_gather(expert_rows, 'seq', axis=0, tiled=True)  49.2 us
    while x4, local copies, waits for them, and re-layouts, shards(): lax.scan(scan_step, state, (jnp.arange(blocks, dtype=jnp.int32), key_stac...  25.5 us
    another operation x1, loops' own time, shards(): lax.scan(scan_step, state, (jnp.arange(blocks, dtype=jnp.int32), key_stac...  20.7 us
  transfers between devices with their start and end apart: 6, of which 6 were waited for; matrix products, arithmetic and copies ran while one was open for 2% of the time, Pallas kernels for 0%

commit v1 on v0

--- a/solution.py
+++ b/solution.py
@@ -101,7 +101,7 @@
         .astype(jnp.bfloat16)
     )
     mixed = jnp.dot(
-        lax.all_gather(attended, "exp", axis=1, tiled=True),
+        jnp.concatenate(lax.all_gather(attended, "exp"), axis=1),
         out_proj,
         preferred_element_type=jnp.float32,
     )

time: 669 us -> 676 us (1.010)
  local copies, waits for them, and re-layouts: 59.3 us -> 66.9 us
where the time goes in v1:
time: 676 us; the launch traced here: 675 us
  waiting for transfers between devices  506 us (75%)
  local copies, waits for them, and re-layouts  66.9 us (10%)
  matrix products  41 us (6%)
  loops' own time  20.9 us (3%)
  blocking collectives  14.6 us (2%)
  between operations  13.7 us (2%)
  other arithmetic  10.7 us (2%)
    all_gather x1, waiting for transfers between devices, shards(): key_piece = lax.all_gather(keys, 'seq', axis=0, tiled=True)  126 us
    all_gather x1, waiting for transfers between devices, shards(): value_piece = lax.all_gather(values, 'seq', axis=0, tiled=True)  113 us
    all_gather x1, waiting for transfers between devices, shards(): lax.all_gather(attended, 'exp')  79.5 us
    reduce_scatter x1, waiting for transfers between devices, shards(): lax.psum_scatter(spread.astype(jnp.bfloat16), 'exp', scatter_dimension=1,...  70.5 us
    reduce_scatter x1, waiting for transfers between devices, shards(): lax.psum_scatter(jnp.dot(inner_act, w_down[0], preferred_element_type=jnp...  66.7 us
    all_gather x1, waiting for transfers between devices, shards(): piece = lax.all_gather(expert_rows, 'seq', axis=0, tiled=True)  49.2 us
    while x4, local copies, waits for them, and re-layouts, shards(): lax.scan(scan_step, state, (jnp.arange(blocks, dtype=jnp.int32), key_stac...  25.5 us
    another operation x1, loops' own time, shards(): lax.scan(scan_step, state, (jnp.arange(blocks, dtype=jnp.int32), key_stac...  20.7 us
  transfers between devices with their start and end apart: 6, of which 6 were waited for; matrix products, arithmetic and copies ran while one was open for 2% of the time, Pallas kernels for 0%

profile of v1, /device:TPU:0, one launch (start us, length us, event | category | flops | bytes accessed | tf_op | source)
XLA Modules:
  0.0 674.6 jit_solution(9337841595333922027)
XLA Ops:
  6.5 0.7 all-gather.5.cloned.1.call-update
  7.3 0.7 all-gather.7.cloned.1.call-update
  8.1 1.5 copy.60
  9.6 0.7 copy.62
  10.2 0.8 dynamic_slice.55
  11.0 125.7 %all-gather.5.cloned.1.call-done = bf16[4096,1024]{1,0:T(8,128)(2,1)} async-done(((bf16[512,1024]{1,0:T(8,128)(2,1)}), bf16[4096,1024]{1,0:T(8,128)(2,1)}) %all-gather.5.cloned.1.call-update) | async-done | bytes 8388624 | tf_op jit(solution)/shard_map/all_gather | solution.py:83
  136.7 11.6 %copy.61 = bf16[8,512,1024]{1,2,0:T(8,128)(2,1)} copy(bf16[8,512,1024]{2,1,0:T(8,128)(2,1)} %bitcast.80) | data formatting | bytes 16777216 | tf_op jit(solution)/shard_map/while | solution.py:94
  148.3 113.2 %all-gather.7.cloned.1.call-done = bf16[4096,1024]{1,0:T(8,128)(2,1)} async-done(((bf16[512,1024]{1,0:T(8,128)(2,1)}), bf16[4096,1024]{1,0:T(8,128)(2,1)}) %all-gather.7.cloned.1.call-update) | async-done | bytes 8388624 | tf_op jit(solution)/shard_map/all_gather | solution.py:84
  261.5 11.4 %copy.63 = bf16[8,512,1024]{1,2,0:T(8,128)(2,1)} copy(bf16[8,512,1024]{2,1,0:T(8,128)(2,1)} %bitcast.81) | data formatting | bytes 16777216 | tf_op jit(solution)/shard_map/while | solution.py:94
  273.1 55.4 %while.18 = (s32[]{:T(128)}, f32[512,8]{0,1:T(8,128)S(1)}, f32[512,8]{0,1:T(8,128)S(1)}, f32[512,8,128]{2,0,1:T(8,128)S(1)}, s32[8]{0:T(128)S(1)}, /*index=5*/s3...) while((s32[]{:T(128)}, f32[512,8]{0,1:T(8,128)S(1)}, ...), condition=%wide.region_5.6_spmd, body=%wide.region_0.5_spmd.sunk | while | flops 1098654208 | bytes 38025672 | solution.py:94
  273.1 0.6 dynamic_slice.64
  274.4 1.3 dynamic_slice.65
  275.6 0.6 slice.33
  277.5 0.6 slice.32
  278.7 9.6 %conditional.2 = (f32[512,8]{0,1:T(8,128)S(1)}, f32[512,8]{0,1:T(8,128)S(1)}, f32[512,8,128]{2,0,1:T(8,128)S(1)}) conditional(s32[]{:T(128)} %convert_element_type.110, (s32[]{:T(128)}, s32[512]{0:T(512)S(1)}, s32[4096]{0:T(1024)}, s32[512]{0:T(512)S(1)}, bf16[8,512,1024]{1,2,0:T(8,128)(2,1)}, /*index=5*/s32[]{:T(128)}, ...), branch_computations={%region_1.3_spmd, %region_4.4_spmd} | conditional | flops 1098654208 | bytes 37992520 | solution.py:70
  278.8 0.8 dynamic_slice.47
  279.8 1.7 constant_dynamic-slice_fusion
  281.5 1.7 fusion.2
  283.2 1.7 fusion.1
  285.0 3.4 bitcast_add_fusion
  288.4 0.6 dynamic_slice.64
  289.6 1.3 dynamic_slice.65
  292.8 0.6 slice.32
  294.1 0.6 dynamic_slice.64
  295.4 1.3 dynamic_slice.65
  296.7 0.6 slice.33
  298.5 0.6 slice.32
  299.8 0.6 dynamic_slice.64
  301.1 1.3 dynamic_slice.65
  302.4 0.6 slice.33
  304.3 0.6 slice.32
  305.6 0.6 dynamic_slice.64
  306.8 1.3 dynamic_slice.65
  308.1 0.6 slice.33
  310.0 0.6 slice.32
  311.3 0.6 dynamic_slice.64
  312.6 1.3 dynamic_slice.65
  315.7 0.6 slice.32
  317.0 0.6 dynamic_slice.64
  318.3 1.3 dynamic_slice.65
  319.6 0.6 slice.33
  321.5 0.6 slice.32
  322.8 0.6 dynamic_slice.64
  324.0 1.3 dynamic_slice.65
  325.3 0.6 slice.33
  327.2 0.6 slice.32
  328.5 1.8 copy.64
  330.3 1.9 divide_convert_fusion
  332.2 1.3 copy.65
  334.6 79.5 %all-gather.9.cloned.1.call-done = bf16[4,512,1024]{2,1,0:T(8,128)(2,1)} async-done(((bf16[1,512,1024]{2,1,0:T(8,128)(2,1)}), bf16[4,512,1024]{2,1,0:T(8,128)(2,1)}) %all-gather.9.cloned.1.call-update) | async-done | bytes 4194320 | tf_op jit(solution)/shard_map/all_gather | solution.py:104
  414.2 6.3 copy.66
  420.5 14.2 %fusion.18 = (f32[512]{0:T(512)S(1)}, bf16[512,2048]{1,0:T(8,128)(2,1)S(1)}) fusion(bf16[512,4096]{0,1:T(8,128)(2,1)} %bitcast.83, bf16[4096,2048]{1,0:T(8,128)(2,1)} %param.22, bf16[512,2048]{1,0:T(8,128)(2,1)} %param.17), kind=kOutput, calls=%fused_computation.30 | convolution fusion | flops 8596226048 | bytes 25167872 | tf_op jit(solution)/shard_map/dot_general | solution.py:103
  434.6 5.9 psum.7
  440.5 2.1 fusion.20
  442.7 2.8 gather_fusion
  446.0 8.7 %all_to_all.5 = bf16[16,4,2048]{2,0,1:T(8,128)(2,1)S(1)} all-to-all(bf16[16,4,2048]{2,0,1:T(8,128)(2,1)S(1)} %fusion.34), channel_id=1, replica_groups=mesh['seq'=8,'exp'=4] {'exp'}, dimensions={1} | all-to-all | bytes 524288 | tf_op jit(solution)/shard_map/all_to_all | solution.py:124
  454.7 0.7 copy.73
  455.5 49.2 %all-gather.11.cloned.1.call-done = bf16[128,8192]{1,0:T(8,128)(2,1)} async-done(((bf16[16,8192]{1,0:T(8,128)(2,1)}), bf16[128,8192]{1,0:T(8,128)(2,1)}) %all-gather.11.cloned.1.call-update) | async-done | bytes 2097168 | tf_op jit(solution)/shard_map/all_gather | solution.py:127
  504.7 5.4 fusion.16
  510.1 9.6 %convolution_convert_fusion.1 = bf16[128,8192]{1,0:T(8,128)(2,1)} fusion(bf16[1,512,8192]{2,1,0:T(8,128)(2,1)} %param.29, bf16[128,8192]{1,0:T(8,128)(2,1)S(1)} %copy-done.1, bf16[1,8192,512]{2,1,0:T(8,128)(2,1)} %param.28, f32[128,512]{1,0:T(8,128)S(1)} %fusion.16), kind=kOutput, calls=%fused_computation.21 | convolution fusion | flops 2148925440 | bytes 21233664 | tf_op jit(solution)/shard_map/dot_general | solution.py:132
  520.3 66.7 %reduce-scatter.3.cloned.1.call-done = bf16[16,8192]{1,0:T(8,128)(2,1)} async-done(((bf16[128,8192]{1,0:T(8,128)(2,1)}), bf16[16,8192]{1,0:T(8,128)(2,1)}) %reduce-scatter.3.cloned.1.call-update) | async-done | bytes 262160 | tf_op jit(solution)/shard_map/reduce_scatter | solution.py:131
  587.0 6.6 convolution_convert_fusion
  593.6 70.5 %reduce-scatter.5.cloned.1.call-done = bf16[512,2048]{1,0:T(8,128)(2,1)} async-done(((bf16[512,8192]{1,0:T(8,128)(2,1)}), bf16[512,2048]{1,0:T(8,128)(2,1)}) %reduce-scatter.5.cloned.1.call-update) | async-done | bytes 2097168 | tf_op jit(solution)/shard_map/reduce_scatter | solution.py:145
  664.1 3.7 fusion.21
  (77 shorter events, 4.0 us)
Async XLA Ops:
  6.5 513.5 %copy-start = (bf16[8192,1]{0,1:T(2,128)(2,1)S(1)}, bf16[8192,1]{0,1:T(2,128)(2,1)}, u32[]{:S(2)}) copy-start(bf16[8192,1]{0,1:T(2,128)(2,1)} %param.26) | copy-start | bytes 49156
  6.5 130.1 %all-gather.5.cloned.1.call-start = ((), (), s32[]{:S(2)}) async-start(), calls=%async_computation.3 | async-start | bytes 9437184 | tf_op jit(solution)/shard_map/all_gather | solution.py:83
  7.3 254.2 %all-gather.7.cloned.1.call-start = ((), (), s32[]{:S(2)}) async-start(), calls=%async_computation.4 | async-start | bytes 9437184 | tf_op jit(solution)/shard_map/all_gather | solution.py:84
  8.0 406.2 %all-gather.9.cloned.1.call-start = ((), (), s32[]{:S(2)}) async-start(), calls=%async_computation.5 | async-start | bytes 5242880 | tf_op jit(solution)/shard_map/all_gather | solution.py:104
  330.3 3.5 copy-start.6
  330.3 4.3 copy-start.7
  330.3 4.3 copy-start.5
  333.6 171.1 %all-gather.11.cloned.1.call-start = ((), (), s32[]{:S(2)}) async-start(), calls=%async_computation.6 | async-start | bytes 2359296 | tf_op jit(solution)/shard_map/all_gather | solution.py:127
  434.6 20.8 %copy-start.2 = (bf16[512,2048]{1,0:T(8,128)(2,1)}, bf16[512,2048]{1,0:T(8,128)(2,1)S(1)}, u32[]{:S(2)}) copy-start(bf16[512,2048]{1,0:T(8,128)(2,1)S(1)} %get-tuple-element.425) | copy-start | bytes 6291460
  455.4 131.6 %reduce-scatter.3.cloned.1.call-start = ((), (), s32[]{:S(2)}) async-start(), calls=%async_computation.7 | async-start | bytes 2359296 | tf_op jit(solution)/shard_map/reduce_scatter | solution.py:131
  504.7 5.4 copy-start.1
  510.1 10.0 %copy-start.4 = (bf16[4,2,8,2048]{3,2,0,1:T(8,128)(2,1)S(1)}, bf16[4,2,8,2048]{3,2,0,1:T(8,128)(2,1)}, u32[]{:S(2)}) copy-start(bf16[4,2,8,2048]{3,2,0,1:T(8,128)(2,1)} %copy.73) | copy-start | bytes 786436
  519.8 144.3 %reduce-scatter.5.cloned.1.call-start = ((), (), s32[]{:S(2)}) async-start(), calls=%async_computation.8 | async-start | bytes 10485760 | tf_op jit(solution)/shard_map/reduce_scatter | solution.py:145
  593.5 70.5 %copy-start.3 = (bf16[512,2048]{1,0:T(8,128)(2,1)S(1)}, bf16[512,2048]{1,0:T(8,128)(2,1)}, u32[]{:S(2)}) copy-start(bf16[512,2048]{1,0:T(8,128)(2,1)} %copy-done.2) | copy-start | bytes 6291460
Sparse Core Ops, SparseCore 0:
  9.5 127.1 all-gather.4
  138.8 122.6 all-gather.6
  333.7 80.4 all-gather.8
  455.5 49.0 all-gather.10
  519.9 67.0 reduce-scatter.2
  593.7 70.3 reduce-scatter.4
